TPU v7x, 32 devices: a whole 2x2x4 slice. The times are simulated.
32 devices in a mesh: scen: 8 (over y, x, core), veh: 4 (over z).
Axes of the slice: x: 2, y: 2, z: 4, core: 2. Of those that a mesh axis runs over, the one named last changes fastest.
Arguments:
- start_plan: bfloat16 [128, 3584, 128], P('scen', 'veh'), may hold values from -6 to 6
- linear_cost: bfloat16 [128, 3584, 128], P('scen', 'veh'), may hold values from -12 to 12
- price: bfloat16 [128, 3584, 128], P('scen', 'veh'), may hold values from -6 to 6
- anchor: bfloat16 [8, 3584, 128], P(None, 'veh'), may hold values from -6 to 6
- hessian: bfloat16 [128, 128, 128], P('scen'), as said below
- usage_coef: bfloat16 [3584, 128], P('veh'), may hold values from -1.5 to 1.5
- crew_limit: float32 [128, 350], P('scen'), may hold values from -48 to 48
- crew_dual: float32 [128, 350], P('scen'), may hold values from 0 to 2
- crew_row: int32 [3584], P('veh'), may hold values from 0 to 349
- bundle_of: int32 [128, 1], replicated, may hold values from 0 to 7
- scen_weight: int32 [128], replicated, may hold values from 1 to 8
Outputs:
- new_plan: bfloat16 [128, 3584, 128], P('scen', 'veh')
- new_price: bfloat16 [128, 3584, 128], P('scen', 'veh')
- bundle_mean: bfloat16 [8, 3584, 128], P('scen', 'veh')
- new_dual: float32 [128, 350], P('scen')
- gap: float32 [], replicated
Inputs may be any that keep to these rules, and one draw needn't show every extreme that they name: `bundle_of`: every bundle holds one scenario or more. `hessian`: symmetric.
All inputs are finite; a program needn't handle non-finite values.
Results may differ from a plain program's by a relative error of at most 0.0013.
The roundings to bfloat16 on the way count: a program that leaves them out, or rounds other values in their place, can miss the bound.
Values sent between devices are 32-bit elements; how exact they have to be, the bound alone decides.
A program may use at most 128 MiB of HBM per device.

v0:
```python
import jax
import jax.numpy as jnp
from jax import lax
from jax.sharding import PartitionSpec as P

ITERS = 12
penalty = 1.0
step_size = 0.02
dual_step = 0.02
highest = lax.Precision.HIGHEST


def shards(
    start_plan,
    linear_cost,
    price,
    anchor,
    hessian,
    usage_coef,
    crew_limit,
    crew_dual,
    crew_row,
    bundle_of,
    scen_weight,
):
    local_scen = start_plan.shape[0]
    bundle_count = anchor.shape[0]
    crew_count = crew_limit.shape[1]
    offset = lax.axis_index("scen") * local_scen
    all_bundles = bundle_of[:, 0]
    my_bundles = lax.dynamic_slice_in_dim(all_bundles, offset, local_scen)
    my_weights = lax.dynamic_slice_in_dim(scen_weight, offset, local_scen).astype(jnp.float32)
    bundle_ids = jnp.arange(bundle_count, dtype=jnp.int32)
    selector = (my_bundles[:, None] == bundle_ids[None, :]).astype(jnp.float32)
    anchored = jnp.einsum(
        "sb,bvi->svi", selector.astype(jnp.bfloat16), anchor, preferred_element_type=jnp.float32
    )
    linear_part = linear_cost.astype(jnp.float32) + price.astype(jnp.float32) - penalty * anchored
    coefficient = usage_coef.astype(jnp.float32)
    crew_map = (crew_row[:, None] == jnp.arange(crew_count, dtype=jnp.int32)[None, :]).astype(
        jnp.float32
    )

    def advance(index, state_pair):
        roster, multiplier = state_pair
        rounded = roster.astype(jnp.bfloat16)
        curvature = jnp.einsum("svi,sij->svj", rounded, hessian, preferred_element_type=jnp.float32)
        consumed = jnp.sum(roster * coefficient[None], axis=2)
        partial_use = jnp.dot(consumed, crew_map, precision=highest)
        usage = lax.psum(partial_use, "veh")
        updated = jnp.maximum(multiplier + dual_step * (usage - crew_limit), 0.0)
        per_vehicle = jnp.dot(multiplier, crew_map.T, precision=highest)
        gradient = (
            curvature + linear_part + penalty * roster + per_vehicle[:, :, None] * coefficient[None]
        )
        return (roster - step_size * gradient, updated)

    roster, multiplier = lax.fori_loop(
        0, ITERS, advance, (start_plan.astype(jnp.float32), crew_dual)
    )
    weighted_pick = selector * my_weights[:, None]
    every_weight = jnp.sum(
        (all_bundles[:, None] == bundle_ids[None, :]).astype(jnp.float32)
        * scen_weight.astype(jnp.float32)[:, None],
        axis=0,
    )
    owned_rows = bundle_count // lax.axis_size("scen")
    own_start = lax.axis_index("scen") * owned_rows
    partial_sums = jnp.einsum("sb,svi->bvi", weighted_pick, roster, precision=highest)
    totals = lax.psum(partial_sums, "scen")
    every_mean = totals / every_weight[:, None, None]
    own_mean = lax.dynamic_slice_in_dim(every_mean, own_start, owned_rows)
    mean_here = jnp.einsum("sb,bvi->svi", selector, every_mean, precision=highest)
    deviation = roster - mean_here
    new_price = (price.astype(jnp.float32) + penalty * deviation).astype(jnp.bfloat16)
    spread = jnp.sum(my_weights * jnp.sum(deviation * deviation, axis=(1, 2)))
    spread_total = lax.psum(spread, ("scen", "veh"))
    entries = start_plan.shape[1] * lax.axis_size("veh") * start_plan.shape[2]
    gap = jnp.sqrt(spread_total / (jnp.sum(scen_weight.astype(jnp.float32)) * entries))
    return (roster.astype(jnp.bfloat16), new_price, own_mean.astype(jnp.bfloat16), multiplier, gap)


def solution(mesh):
    return jax.shard_map(
        shards,
        mesh=mesh,
        in_specs=(
            P("scen", "veh", None),
            P("scen", "veh", None),
            P("scen", "veh", None),
            P(None, "veh", None),
            P("scen", None, None),
            P("veh", None),
            P("scen", None),
            P("scen", None),
            P("veh"),
            P(),
            P(),
        ),
        out_specs=(
            P("scen", "veh", None),
            P("scen", "veh", None),
            P("scen", "veh", None),
            P("scen", None),
            P(),
        ),
        check_vma=False,
    )
```

profile of v0, /device:TPU:0, one launch (start us, length us, event | category | flops | bytes accessed | tf_op | source)
XLA Modules:
  0.0 568.2 jit_solution(2180171724463665782)
XLA Ops:
  8.7 22.6 %fusion.12 = f32[16,896,128]{2,0,1:T(8,128)S(1)} fusion(bf16[16,896,128]{2,1,0:T(8,128)(2,1)} %param.14, bf16[16,896,128]{2,1,0:T(8,128)(2,1)} %param.15, bf16[8,896,128]{2,1,0:T(8,128)(2,1)S(1)} %copy-done, s32[16]{0:T(128)S(1)} %dynamic-slice_bitcast_fusion), kind=kOutput, calls=%fused_computation.15 | convolution fusion | flops 36700544 | bytes 16515136 | tf_op jit(solution)/shard_map/sb,bvi->svi/dot_general | solution.py:35
  31.3 5.2 copy.27
  40.4 364.3 %while.13 = (s32[]{:T(128)}, f32[16,896,128]{2,1,0:T(8,128)}, f32[16,350]{1,0:T(8,128)S(1)}, bf16[16,128,128]{2,1,0:T(8,128)(2,1)S(1)}, f32[16,896,128]{2,1,0:T(...) while((s32[]{:T(128)}, f32[16,896,128]{2,1,0:T(8,128)}, ...), condition=%wide.region_3.0_spmd.clone, body=%wide.region_0.0_spmd.clone.sunk | while | flops 607967616 | bytes 75257976 | solution.py:58
  47.0 5.9 %multiply_subtract_fusion.2 = f32[16,896,128]{2,1,0:T(8,128)} fusion(f32[16,896,128]{2,1,0:T(8,128)S(1)} %copy.53, f32[16,896,128]{2,1,0:T(8,128)S(1)} %copy-done.1, f32[896,128]{1,0:T(8,128)S(1)} %get-tuple-element.185, f32[16,896]{1,0:T(8,128)S(1)} %fusion.47, bf16[16,128,128]{2,1,0:T(8,128)(2,1)S(1)} %get-tuple-element.183), kind=kOutput, calls=%fused_computation.2.clone.1 | convolution fusion | flops 482607104 | bytes 23060480 | tf_op jit(solution)/shard_map/while/body/eval_jaxpr/svi,sij->svj/dot_general | solution.py:47
  53.8 20.8 %psum.25 = f32[16,350]{1,0:T(8,128)S(1)} all-reduce(f32[16,350]{1,0:T(8,128)S(1)} %fusion.48), channel_id=1, replica_groups=mesh['scen'=8,'veh'=4] {'veh'}, use_global_device_ids=true, to_apply=%region_2.0 | all-reduce | flops 5600 | bytes 44800 | tf_op jit(solution)/shard_map/while/body/eval_jaxpr/psum | solution.py:50
  81.1 5.9 %multiply_subtract_fusion.2 = f32[16,896,128]{2,1,0:T(8,128)} fusion(f32[16,896,128]{2,1,0:T(8,128)S(1)} %copy.53, f32[16,896,128]{2,1,0:T(8,128)S(1)} %copy-done.1, f32[896,128]{1,0:T(8,128)S(1)} %get-tuple-element.185, f32[16,896]{1,0:T(8,128)S(1)} %fusion.47, bf16[16,128,128]{2,1,0:T(8,128)(2,1)S(1)} %get-tuple-element.183), kind=kOutput, calls=%fused_computation.2.clone.1 | convolution fusion | flops 482607104 | bytes 23060480 | tf_op jit(solution)/shard_map/while/body/eval_jaxpr/svi,sij->svj/dot_general | solution.py:47
  88.0 15.8 %psum.25 = f32[16,350]{1,0:T(8,128)S(1)} all-reduce(f32[16,350]{1,0:T(8,128)S(1)} %fusion.48), channel_id=1, replica_groups=mesh['scen'=8,'veh'=4] {'veh'}, use_global_device_ids=true, to_apply=%region_2.0 | all-reduce | flops 5600 | bytes 44800 | tf_op jit(solution)/shard_map/while/body/eval_jaxpr/psum | solution.py:50
  110.4 5.9 %multiply_subtract_fusion.2 = f32[16,896,128]{2,1,0:T(8,128)} fusion(f32[16,896,128]{2,1,0:T(8,128)S(1)} %copy.53, f32[16,896,128]{2,1,0:T(8,128)S(1)} %copy-done.1, f32[896,128]{1,0:T(8,128)S(1)} %get-tuple-element.185, f32[16,896]{1,0:T(8,128)S(1)} %fusion.47, bf16[16,128,128]{2,1,0:T(8,128)(2,1)S(1)} %get-tuple-element.183), kind=kOutput, calls=%fused_computation.2.clone.1 | convolution fusion | flops 482607104 | bytes 23060480 | tf_op jit(solution)/shard_map/while/body/eval_jaxpr/svi,sij->svj/dot_general | solution.py:47
  117.2 17.4 %psum.25 = f32[16,350]{1,0:T(8,128)S(1)} all-reduce(f32[16,350]{1,0:T(8,128)S(1)} %fusion.48), channel_id=1, replica_groups=mesh['scen'=8,'veh'=4] {'veh'}, use_global_device_ids=true, to_apply=%region_2.0 | all-reduce | flops 5600 | bytes 44800 | tf_op jit(solution)/shard_map/while/body/eval_jaxpr/psum | solution.py:50
  141.2 5.9 %multiply_subtract_fusion.2 = f32[16,896,128]{2,1,0:T(8,128)} fusion(f32[16,896,128]{2,1,0:T(8,128)S(1)} %copy.53, f32[16,896,128]{2,1,0:T(8,128)S(1)} %copy-done.1, f32[896,128]{1,0:T(8,128)S(1)} %get-tuple-element.185, f32[16,896]{1,0:T(8,128)S(1)} %fusion.47, bf16[16,128,128]{2,1,0:T(8,128)(2,1)S(1)} %get-tuple-element.183), kind=kOutput, calls=%fused_computation.2.clone.1 | convolution fusion | flops 482607104 | bytes 23060480 | tf_op jit(solution)/shard_map/while/body/eval_jaxpr/svi,sij->svj/dot_general | solution.py:47
  148.1 15.8 %psum.25 = f32[16,350]{1,0:T(8,128)S(1)} all-reduce(f32[16,350]{1,0:T(8,128)S(1)} %fusion.48), channel_id=1, replica_groups=mesh['scen'=8,'veh'=4] {'veh'}, use_global_device_ids=true, to_apply=%region_2.0 | all-reduce | flops 5600 | bytes 44800 | tf_op jit(solution)/shard_map/while/body/eval_jaxpr/psum | solution.py:50
  170.5 5.9 %multiply_subtract_fusion.2 = f32[16,896,128]{2,1,0:T(8,128)} fusion(f32[16,896,128]{2,1,0:T(8,128)S(1)} %copy.53, f32[16,896,128]{2,1,0:T(8,128)S(1)} %copy-done.1, f32[896,128]{1,0:T(8,128)S(1)} %get-tuple-element.185, f32[16,896]{1,0:T(8,128)S(1)} %fusion.47, bf16[16,128,128]{2,1,0:T(8,128)(2,1)S(1)} %get-tuple-element.183), kind=kOutput, calls=%fused_computation.2.clone.1 | convolution fusion | flops 482607104 | bytes 23060480 | tf_op jit(solution)/shard_map/while/body/eval_jaxpr/svi,sij->svj/dot_general | solution.py:47
  177.3 17.4 %psum.25 = f32[16,350]{1,0:T(8,128)S(1)} all-reduce(f32[16,350]{1,0:T(8,128)S(1)} %fusion.48), channel_id=1, replica_groups=mesh['scen'=8,'veh'=4] {'veh'}, use_global_device_ids=true, to_apply=%region_2.0 | all-reduce | flops 5600 | bytes 44800 | tf_op jit(solution)/shard_map/while/body/eval_jaxpr/psum | solution.py:50
  201.3 5.9 %multiply_subtract_fusion.2 = f32[16,896,128]{2,1,0:T(8,128)} fusion(f32[16,896,128]{2,1,0:T(8,128)S(1)} %copy.53, f32[16,896,128]{2,1,0:T(8,128)S(1)} %copy-done.1, f32[896,128]{1,0:T(8,128)S(1)} %get-tuple-element.185, f32[16,896]{1,0:T(8,128)S(1)} %fusion.47, bf16[16,128,128]{2,1,0:T(8,128)(2,1)S(1)} %get-tuple-element.183), kind=kOutput, calls=%fused_computation.2.clone.1 | convolution fusion | flops 482607104 | bytes 23060480 | tf_op jit(solution)/shard_map/while/body/eval_jaxpr/svi,sij->svj/dot_general | solution.py:47
  208.2 16.0 %psum.25 = f32[16,350]{1,0:T(8,128)S(1)} all-reduce(f32[16,350]{1,0:T(8,128)S(1)} %fusion.48), channel_id=1, replica_groups=mesh['scen'=8,'veh'=4] {'veh'}, use_global_device_ids=true, to_apply=%region_2.0 | all-reduce | flops 5600 | bytes 44800 | tf_op jit(solution)/shard_map/while/body/eval_jaxpr/psum | solution.py:50
  230.7 5.9 %multiply_subtract_fusion.2 = f32[16,896,128]{2,1,0:T(8,128)} fusion(f32[16,896,128]{2,1,0:T(8,128)S(1)} %copy.53, f32[16,896,128]{2,1,0:T(8,128)S(1)} %copy-done.1, f32[896,128]{1,0:T(8,128)S(1)} %get-tuple-element.185, f32[16,896]{1,0:T(8,128)S(1)} %fusion.47, bf16[16,128,128]{2,1,0:T(8,128)(2,1)S(1)} %get-tuple-element.183), kind=kOutput, calls=%fused_computation.2.clone.1 | convolution fusion | flops 482607104 | bytes 23060480 | tf_op jit(solution)/shard_map/while/body/eval_jaxpr/svi,sij->svj/dot_general | solution.py:47
  237.5 17.3 %psum.25 = f32[16,350]{1,0:T(8,128)S(1)} all-reduce(f32[16,350]{1,0:T(8,128)S(1)} %fusion.48), channel_id=1, replica_groups=mesh['scen'=8,'veh'=4] {'veh'}, use_global_device_ids=true, to_apply=%region_2.0 | all-reduce | flops 5600 | bytes 44800 | tf_op jit(solution)/shard_map/while/body/eval_jaxpr/psum | solution.py:50
  261.4 5.9 %multiply_subtract_fusion.2 = f32[16,896,128]{2,1,0:T(8,128)} fusion(f32[16,896,128]{2,1,0:T(8,128)S(1)} %copy.53, f32[16,896,128]{2,1,0:T(8,128)S(1)} %copy-done.1, f32[896,128]{1,0:T(8,128)S(1)} %get-tuple-element.185, f32[16,896]{1,0:T(8,128)S(1)} %fusion.47, bf16[16,128,128]{2,1,0:T(8,128)(2,1)S(1)} %get-tuple-element.183), kind=kOutput, calls=%fused_computation.2.clone.1 | convolution fusion | flops 482607104 | bytes 23060480 | tf_op jit(solution)/shard_map/while/body/eval_jaxpr/svi,sij->svj/dot_general | solution.py:47
  268.3 16.1 %psum.25 = f32[16,350]{1,0:T(8,128)S(1)} all-reduce(f32[16,350]{1,0:T(8,128)S(1)} %fusion.48), channel_id=1, replica_groups=mesh['scen'=8,'veh'=4] {'veh'}, use_global_device_ids=true, to_apply=%region_2.0 | all-reduce | flops 5600 | bytes 44800 | tf_op jit(solution)/shard_map/while/body/eval_jaxpr/psum | solution.py:50
  291.0 5.9 %multiply_subtract_fusion.2 = f32[16,896,128]{2,1,0:T(8,128)} fusion(f32[16,896,128]{2,1,0:T(8,128)S(1)} %copy.53, f32[16,896,128]{2,1,0:T(8,128)S(1)} %copy-done.1, f32[896,128]{1,0:T(8,128)S(1)} %get-tuple-element.185, f32[16,896]{1,0:T(8,128)S(1)} %fusion.47, bf16[16,128,128]{2,1,0:T(8,128)(2,1)S(1)} %get-tuple-element.183), kind=kOutput, calls=%fused_computation.2.clone.1 | convolution fusion | flops 482607104 | bytes 23060480 | tf_op jit(solution)/shard_map/while/body/eval_jaxpr/svi,sij->svj/dot_general | solution.py:47
  297.8 17.1 %psum.25 = f32[16,350]{1,0:T(8,128)S(1)} all-reduce(f32[16,350]{1,0:T(8,128)S(1)} %fusion.48), channel_id=1, replica_groups=mesh['scen'=8,'veh'=4] {'veh'}, use_global_device_ids=true, to_apply=%region_2.0 | all-reduce | flops 5600 | bytes 44800 | tf_op jit(solution)/shard_map/while/body/eval_jaxpr/psum | solution.py:50
  321.5 5.9 %multiply_subtract_fusion.2 = f32[16,896,128]{2,1,0:T(8,128)} fusion(f32[16,896,128]{2,1,0:T(8,128)S(1)} %copy.53, f32[16,896,128]{2,1,0:T(8,128)S(1)} %copy-done.1, f32[896,128]{1,0:T(8,128)S(1)} %get-tuple-element.185, f32[16,896]{1,0:T(8,128)S(1)} %fusion.47, bf16[16,128,128]{2,1,0:T(8,128)(2,1)S(1)} %get-tuple-element.183), kind=kOutput, calls=%fused_computation.2.clone.1 | convolution fusion | flops 482607104 | bytes 23060480 | tf_op jit(solution)/shard_map/while/body/eval_jaxpr/svi,sij->svj/dot_general | solution.py:47
  328.4 16.2 %psum.25 = f32[16,350]{1,0:T(8,128)S(1)} all-reduce(f32[16,350]{1,0:T(8,128)S(1)} %fusion.48), channel_id=1, replica_groups=mesh['scen'=8,'veh'=4] {'veh'}, use_global_device_ids=true, to_apply=%region_2.0 | all-reduce | flops 5600 | bytes 44800 | tf_op jit(solution)/shard_map/while/body/eval_jaxpr/psum | solution.py:50
  351.1 5.9 %multiply_subtract_fusion.2 = f32[16,896,128]{2,1,0:T(8,128)} fusion(f32[16,896,128]{2,1,0:T(8,128)S(1)} %copy.53, f32[16,896,128]{2,1,0:T(8,128)S(1)} %copy-done.1, f32[896,128]{1,0:T(8,128)S(1)} %get-tuple-element.185, f32[16,896]{1,0:T(8,128)S(1)} %fusion.47, bf16[16,128,128]{2,1,0:T(8,128)(2,1)S(1)} %get-tuple-element.183), kind=kOutput, calls=%fused_computation.2.clone.1 | convolution fusion | flops 482607104 | bytes 23060480 | tf_op jit(solution)/shard_map/while/body/eval_jaxpr/svi,sij->svj/dot_general | solution.py:47
  358.0 17.1 %psum.25 = f32[16,350]{1,0:T(8,128)S(1)} all-reduce(f32[16,350]{1,0:T(8,128)S(1)} %fusion.48), channel_id=1, replica_groups=mesh['scen'=8,'veh'=4] {'veh'}, use_global_device_ids=true, to_apply=%region_2.0 | all-reduce | flops 5600 | bytes 44800 | tf_op jit(solution)/shard_map/while/body/eval_jaxpr/psum | solution.py:50
  381.6 5.9 %multiply_subtract_fusion.2 = f32[16,896,128]{2,1,0:T(8,128)} fusion(f32[16,896,128]{2,1,0:T(8,128)S(1)} %copy.53, f32[16,896,128]{2,1,0:T(8,128)S(1)} %copy-done.1, f32[896,128]{1,0:T(8,128)S(1)} %get-tuple-element.185, f32[16,896]{1,0:T(8,128)S(1)} %fusion.47, bf16[16,128,128]{2,1,0:T(8,128)(2,1)S(1)} %get-tuple-element.183), kind=kOutput, calls=%fused_computation.2.clone.1 | convolution fusion | flops 482607104 | bytes 23060480 | tf_op jit(solution)/shard_map/while/body/eval_jaxpr/svi,sij->svj/dot_general | solution.py:47
  388.5 16.2 %psum.25 = f32[16,350]{1,0:T(8,128)S(1)} all-reduce(f32[16,350]{1,0:T(8,128)S(1)} %fusion.48), channel_id=1, replica_groups=mesh['scen'=8,'veh'=4] {'veh'}, use_global_device_ids=true, to_apply=%region_2.0 | all-reduce | flops 5600 | bytes 44800 | tf_op jit(solution)/shard_map/while/body/eval_jaxpr/psum | solution.py:50
  404.8 14.0 %fusion.14 = f32[8,896,128]{2,0,1:T(8,128)} fusion(f32[16,896,128]{2,1,0:T(8,128)} %get-tuple-element.48, f32[16]{0:T(128)S(1)} %dynamic-slice_convert_fusion.1, s32[16]{0:T(128)S(1)} %dynamic-slice_bitcast_fusion), kind=kOutput, calls=%fused_computation.18 | convolution fusion | flops 176161024 | bytes 11010176 | tf_op jit(solution)/shard_map/sb,svi->bvi/dot_general | solution.py:69
  418.8 5.6 convert_element_type.49
  425.8 67.3 %all-reduce.2.cloned.1.call-done = f32[8,896,128]{2,0,1:T(8,128)} async-done(((f32[8,896,128]{2,0,1:T(8,128)}), f32[8,896,128]{2,0,1:T(8,128)}) %all-reduce.2.cloned.1.call-update) | async-done | bytes 3670032 | tf_op jit(solution)/shard_map/psum | solution.py:70
  496.2 17.2 %multiply_reduce_fusion.1 = (f32[16]{0:T(128)S(1)}, bf16[16,896,128]{2,0,1:T(8,128)(2,1)S(1)}) fusion(bf16[16,896,128]{2,1,0:T(8,128)(2,1)S(1)} %copy-done.3, f32[8,896,128]{2,0,1:T(8,128)S(1)} %broadcast_divide_fusion, s32[16]{0:T(128)S(1)} %dynamic-slice_bitcast_fusion, f32[16,896,128]{2,1,0:T(8,128)} %get-tuple-element.48), kind=kOutput, calls=%fused_computation.17 | convolution fusion | flops 187170928 | bytes 18350208 | tf_op jit(solution)/shard_map/sb,bvi->svi/dot_general | solution.py:73
  516.9 39.5 %psum.22 = f32[]{:T(128)} all-reduce(f32[]{:T(128)} %multiply_reduce_fusion.2), channel_id=1, replica_groups=mesh['scen'=8,'veh'=4] {'scen','veh'}, use_global_device_ids=true, to_apply=%region_8.0 | all-reduce | flops 1 | bytes 8 | tf_op jit(solution)/shard_map/psum | solution.py:77
  (122 shorter events, 106.0 us)
Async XLA Ops:
  7.2 1.5 copy-start
  7.2 485.9 %all-reduce.2.cloned.1.call-start = ((), (), s32[]{:S(2)}) async-start(), calls=%async_computation | async-start | bytes 7340032 | tf_op jit(solution)/shard_map/psum | solution.py:70
  31.3 5.2 copy-start.5
  36.5 3.8 copy-start.9
  36.5 3.8 copy-start.4
  36.5 3.9 copy-start.7
  36.5 3.9 copy-start.8
  36.5 3.9 copy-start.11
  40.4 364.3 %copy-start.10 = (s32[128]{0:T(128)S(1)}, s32[128]{0:T(128)}, u32[]{:S(2)}) copy-start(s32[128]{0:T(128)} %param.23) | copy-start | bytes 1540
  43.5 3.5 copy-start.1
  77.7 3.5 copy-start.1
  106.9 3.5 copy-start.1
  137.8 3.5 copy-start.1
  167.0 3.5 copy-start.1
  197.9 3.5 copy-start.1
  227.2 3.5 copy-start.1
  258.0 3.5 copy-start.1
  287.5 3.5 copy-start.1
  318.1 3.5 copy-start.1
  347.7 3.5 copy-start.1
  378.1 3.5 copy-start.1
  404.7 14.1 %copy-start.6 = (f32[16,350]{1,0:T(8,128)}, f32[16,350]{1,0:T(8,128)S(1)}, u32[]{:S(2)}) copy-start(f32[16,350]{1,0:T(8,128)S(1)} %get-tuple-element.93) | copy-start | bytes 67204
  418.7 6.9 %copy-start.12 = (s32[128,1]{0,1:T(1,128)S(1)}, s32[128,1]{0,1:T(1,128)}, u32[]{:S(2)}) copy-start(s32[128,1]{0,1:T(1,128)} %param.22) | copy-start | bytes 1540
  493.1 3.1 copy-start.3
  496.2 17.2 %copy-start.2 = (f32[8,896,128]{2,0,1:T(8,128)}, f32[8,896,128]{2,0,1:T(8,128)S(1)}, u32[]{:S(2)}) copy-start(f32[8,896,128]{2,0,1:T(8,128)S(1)} %broadcast_divide_fusion) | copy-start | bytes 11010052
Sparse Core Ops, SparseCore 0:
  418.9 74.1 all-reduce.1
where the time goes:
time: 569 us; the launch traced here: 568 us
  blocking collectives  243 us (43%)
  matrix products  152 us (27%)
  waiting for transfers between devices  67.3 us (12%)
  local copies, waits for them, and re-layouts  50.3 us (9%)
  other arithmetic  38.6 us (7%)
  between operations  16.7 us (3%)
    psum x12, blocking collectives, advance(): usage = lax.psum(partial_use, 'veh')  203 us
    dot_general x12, matrix products, advance(): jnp.einsum('svi,sij->svj', rounded, hessian, preferred_element_type=jnp.f...  70.6 us
    psum x1, waiting for transfers between devices, shards(): totals = lax.psum(partial_sums, 'scen')  67.3 us
    psum x1, blocking collectives, shards(): spread_total = lax.psum(spread, ('scen', 'veh'))  39.5 us
    while x36, local copies, waits for them, and re-layouts  37.1 us
    reduce_sum x12, other arithmetic, advance(): consumed = jnp.sum(roster * coefficient[None], axis=2)  25.1 us
    dot_general x1, matrix products, shards(): jnp.einsum('sb,bvi->svi', selector.astype(jnp.bfloat16), anchor, preferre...  22.6 us
    dot_general x1, matrix products, shards(): jnp.einsum('sb,bvi->svi', selector, every_mean, precision=highest)  17.2 us
  transfers between devices with their start and end apart: 1, of which 1 were waited for; matrix products, arithmetic and copies ran while one was open for 1% of the time, Pallas kernels for 0%

commit v1 on v0

--- a/solution.py
+++ b/solution.py
@@ -47,7 +47,7 @@
         curvature = jnp.einsum("svi,sij->svj", rounded, hessian, preferred_element_type=jnp.float32)
         consumed = jnp.sum(roster * coefficient[None], axis=2)
         partial_use = jnp.dot(consumed, crew_map, precision=highest)
-        usage = lax.psum(partial_use, "veh")
+        usage = jnp.sum(lax.all_gather(partial_use, "veh"), axis=0)
         updated = jnp.maximum(multiplier + dual_step * (usage - crew_limit), 0.0)
         per_vehicle = jnp.dot(multiplier, crew_map.T, precision=highest)
         gradient = (

time: 569 us -> 529 us (0.930)
  blocking collectives: 243 us -> 201 us
    psum x12 -> x0, blocking collectives: 203 us -> none  [advance(): usage = lax.psum(partial_use, 'veh')]
    all_gather x0 -> x12, blocking collectives: none -> 162 us  [advance(): usage = jnp.sum(lax.all_gather(partial_use, 'veh'), axis=0)]
where the time goes in v1:
time: 529 us
  blocking collectives  201 us (38%)
  matrix products  152 us (29%)
  waiting for transfers between devices  69.1 us (13%)
  local copies, waits for them, and re-layouts  50.3 us (10%)
  other arithmetic  38.7 us (7%)
  between operations  16.7 us (3%)
    all_gather x12, blocking collectives, advance(): usage = jnp.sum(lax.all_gather(partial_use, 'veh'), axis=0)  162 us
    dot_general x12, matrix products, advance(): jnp.einsum('svi,sij->svj', rounded, hessian, preferred_element_type=jnp.f...  70.6 us
    psum x1, waiting for transfers between devices, shards(): totals = lax.psum(partial_sums, 'scen')  69 us
    psum x1, blocking collectives, shards(): spread_total = lax.psum(spread, ('scen', 'veh'))  39.5 us
    while x36, local copies, waits for them, and re-layouts  37.1 us
    reduce_sum x12, other arithmetic, advance(): consumed = jnp.sum(roster * coefficient[None], axis=2)  25.1 us
    dot_general x1, matrix products, shards(): jnp.einsum('sb,bvi->svi', selector.astype(jnp.bfloat16), anchor, preferre...  22.6 us
    dot_general x1, matrix products, shards(): jnp.einsum('sb,bvi->svi', selector, every_mean, precision=highest)  17.2 us
  transfers between devices with their start and end apart: 1, of which 1 were waited for; matrix products, arithmetic and copies ran while one was open for 1% of the time, Pallas kernels for 0%

profile of v1, /device:TPU:0, one launch (start us, length us, event | category | flops | bytes accessed | tf_op | source)
XLA Modules:
  0.0 528.5 jit_solution(768491632789741028)
XLA Ops:
  8.7 22.6 %fusion.12 = f32[16,896,128]{2,0,1:T(8,128)S(1)} fusion(bf16[16,896,128]{2,1,0:T(8,128)(2,1)} %param.14, bf16[16,896,128]{2,1,0:T(8,128)(2,1)} %param.15, bf16[8,896,128]{2,1,0:T(8,128)(2,1)S(1)} %copy-done, s32[16]{0:T(128)S(1)} %dynamic-slice_bitcast_fusion), kind=kOutput, calls=%fused_computation.15 | convolution fusion | flops 36700544 | bytes 16515136 | tf_op jit(solution)/shard_map/sb,bvi->svi/dot_general | solution.py:35
  31.3 5.2 copy.27
  40.4 322.9 %while.13 = (s32[]{:T(128)}, f32[16,896,128]{2,1,0:T(8,128)}, f32[16,350]{1,0:T(8,128)S(1)}, bf16[16,128,128]{2,1,0:T(8,128)(2,1)S(1)}, f32[16,896,128]{2,1,0:T(...) while((s32[]{:T(128)}, f32[16,896,128]{2,1,0:T(8,128)}, ...), condition=%wide.region_3.0_spmd.clone, body=%wide.region_0.0_spmd.clone.sunk | while | flops 607978752 | bytes 75437192 | solution.py:58
  47.0 5.9 %multiply_subtract_fusion.2 = f32[16,896,128]{2,1,0:T(8,128)} fusion(f32[16,896,128]{2,1,0:T(8,128)S(1)} %copy.53, f32[16,896,128]{2,1,0:T(8,128)S(1)} %copy-done.1, f32[896,128]{1,0:T(8,128)S(1)} %get-tuple-element.187, f32[16,896]{1,0:T(8,128)S(1)} %fusion.47, bf16[16,128,128]{2,1,0:T(8,128)(2,1)S(1)} %get-tuple-element.185), kind=kOutput, calls=%fused_computation.2.clone.1 | convolution fusion | flops 482607104 | bytes 23060480 | tf_op jit(solution)/shard_map/while/body/eval_jaxpr/svi,sij->svj/dot_general | solution.py:47
  53.8 15.1 %all-gather.3 = f32[64,350]{1,0:T(8,128)S(1)} all-gather(f32[16,350]{1,0:T(8,128)S(1)} %fusion.48), channel_id=2, replica_groups=mesh['scen'=8,'veh'=4] {'veh'}, dimensions={0}, use_global_device_ids=true | all-gather | bytes 112000 | tf_op jit(solution)/shard_map/while/body/eval_jaxpr/all_gather | solution.py:50
  75.5 5.9 %multiply_subtract_fusion.2 = f32[16,896,128]{2,1,0:T(8,128)} fusion(f32[16,896,128]{2,1,0:T(8,128)S(1)} %copy.53, f32[16,896,128]{2,1,0:T(8,128)S(1)} %copy-done.1, f32[896,128]{1,0:T(8,128)S(1)} %get-tuple-element.187, f32[16,896]{1,0:T(8,128)S(1)} %fusion.47, bf16[16,128,128]{2,1,0:T(8,128)(2,1)S(1)} %get-tuple-element.185), kind=kOutput, calls=%fused_computation.2.clone.1 | convolution fusion | flops 482607104 | bytes 23060480 | tf_op jit(solution)/shard_map/while/body/eval_jaxpr/svi,sij->svj/dot_general | solution.py:47
  82.3 13.5 %all-gather.3 = f32[64,350]{1,0:T(8,128)S(1)} all-gather(f32[16,350]{1,0:T(8,128)S(1)} %fusion.48), channel_id=2, replica_groups=mesh['scen'=8,'veh'=4] {'veh'}, dimensions={0}, use_global_device_ids=true | all-gather | bytes 112000 | tf_op jit(solution)/shard_map/while/body/eval_jaxpr/all_gather | solution.py:50
  102.4 5.9 %multiply_subtract_fusion.2 = f32[16,896,128]{2,1,0:T(8,128)} fusion(f32[16,896,128]{2,1,0:T(8,128)S(1)} %copy.53, f32[16,896,128]{2,1,0:T(8,128)S(1)} %copy-done.1, f32[896,128]{1,0:T(8,128)S(1)} %get-tuple-element.187, f32[16,896]{1,0:T(8,128)S(1)} %fusion.47, bf16[16,128,128]{2,1,0:T(8,128)(2,1)S(1)} %get-tuple-element.185), kind=kOutput, calls=%fused_computation.2.clone.1 | convolution fusion | flops 482607104 | bytes 23060480 | tf_op jit(solution)/shard_map/while/body/eval_jaxpr/svi,sij->svj/dot_general | solution.py:47
  109.2 13.2 %all-gather.3 = f32[64,350]{1,0:T(8,128)S(1)} all-gather(f32[16,350]{1,0:T(8,128)S(1)} %fusion.48), channel_id=2, replica_groups=mesh['scen'=8,'veh'=4] {'veh'}, dimensions={0}, use_global_device_ids=true | all-gather | bytes 112000 | tf_op jit(solution)/shard_map/while/body/eval_jaxpr/all_gather | solution.py:50
  129.0 5.9 %multiply_subtract_fusion.2 = f32[16,896,128]{2,1,0:T(8,128)} fusion(f32[16,896,128]{2,1,0:T(8,128)S(1)} %copy.53, f32[16,896,128]{2,1,0:T(8,128)S(1)} %copy-done.1, f32[896,128]{1,0:T(8,128)S(1)} %get-tuple-element.187, f32[16,896]{1,0:T(8,128)S(1)} %fusion.47, bf16[16,128,128]{2,1,0:T(8,128)(2,1)S(1)} %get-tuple-element.185), kind=kOutput, calls=%fused_computation.2.clone.1 | convolution fusion | flops 482607104 | bytes 23060480 | tf_op jit(solution)/shard_map/while/body/eval_jaxpr/svi,sij->svj/dot_general | solution.py:47
  135.9 13.3 %all-gather.3 = f32[64,350]{1,0:T(8,128)S(1)} all-gather(f32[16,350]{1,0:T(8,128)S(1)} %fusion.48), channel_id=2, replica_groups=mesh['scen'=8,'veh'=4] {'veh'}, dimensions={0}, use_global_device_ids=true | all-gather | bytes 112000 | tf_op jit(solution)/shard_map/while/body/eval_jaxpr/all_gather | solution.py:50
  155.8 5.9 %multiply_subtract_fusion.2 = f32[16,896,128]{2,1,0:T(8,128)} fusion(f32[16,896,128]{2,1,0:T(8,128)S(1)} %copy.53, f32[16,896,128]{2,1,0:T(8,128)S(1)} %copy-done.1, f32[896,128]{1,0:T(8,128)S(1)} %get-tuple-element.187, f32[16,896]{1,0:T(8,128)S(1)} %fusion.47, bf16[16,128,128]{2,1,0:T(8,128)(2,1)S(1)} %get-tuple-element.185), kind=kOutput, calls=%fused_computation.2.clone.1 | convolution fusion | flops 482607104 | bytes 23060480 | tf_op jit(solution)/shard_map/while/body/eval_jaxpr/svi,sij->svj/dot_general | solution.py:47
  162.6 13.3 %all-gather.3 = f32[64,350]{1,0:T(8,128)S(1)} all-gather(f32[16,350]{1,0:T(8,128)S(1)} %fusion.48), channel_id=2, replica_groups=mesh['scen'=8,'veh'=4] {'veh'}, dimensions={0}, use_global_device_ids=true | all-gather | bytes 112000 | tf_op jit(solution)/shard_map/while/body/eval_jaxpr/all_gather | solution.py:50
  182.6 5.9 %multiply_subtract_fusion.2 = f32[16,896,128]{2,1,0:T(8,128)} fusion(f32[16,896,128]{2,1,0:T(8,128)S(1)} %copy.53, f32[16,896,128]{2,1,0:T(8,128)S(1)} %copy-done.1, f32[896,128]{1,0:T(8,128)S(1)} %get-tuple-element.187, f32[16,896]{1,0:T(8,128)S(1)} %fusion.47, bf16[16,128,128]{2,1,0:T(8,128)(2,1)S(1)} %get-tuple-element.185), kind=kOutput, calls=%fused_computation.2.clone.1 | convolution fusion | flops 482607104 | bytes 23060480 | tf_op jit(solution)/shard_map/while/body/eval_jaxpr/svi,sij->svj/dot_general | solution.py:47
  189.4 13.3 %all-gather.3 = f32[64,350]{1,0:T(8,128)S(1)} all-gather(f32[16,350]{1,0:T(8,128)S(1)} %fusion.48), channel_id=2, replica_groups=mesh['scen'=8,'veh'=4] {'veh'}, dimensions={0}, use_global_device_ids=true | all-gather | bytes 112000 | tf_op jit(solution)/shard_map/while/body/eval_jaxpr/all_gather | solution.py:50
  209.3 5.9 %multiply_subtract_fusion.2 = f32[16,896,128]{2,1,0:T(8,128)} fusion(f32[16,896,128]{2,1,0:T(8,128)S(1)} %copy.53, f32[16,896,128]{2,1,0:T(8,128)S(1)} %copy-done.1, f32[896,128]{1,0:T(8,128)S(1)} %get-tuple-element.187, f32[16,896]{1,0:T(8,128)S(1)} %fusion.47, bf16[16,128,128]{2,1,0:T(8,128)(2,1)S(1)} %get-tuple-element.185), kind=kOutput, calls=%fused_computation.2.clone.1 | convolution fusion | flops 482607104 | bytes 23060480 | tf_op jit(solution)/shard_map/while/body/eval_jaxpr/svi,sij->svj/dot_general | solution.py:47
  216.1 13.3 %all-gather.3 = f32[64,350]{1,0:T(8,128)S(1)} all-gather(f32[16,350]{1,0:T(8,128)S(1)} %fusion.48), channel_id=2, replica_groups=mesh['scen'=8,'veh'=4] {'veh'}, dimensions={0}, use_global_device_ids=true | all-gather | bytes 112000 | tf_op jit(solution)/shard_map/while/body/eval_jaxpr/all_gather | solution.py:50
  236.0 5.9 %multiply_subtract_fusion.2 = f32[16,896,128]{2,1,0:T(8,128)} fusion(f32[16,896,128]{2,1,0:T(8,128)S(1)} %copy.53, f32[16,896,128]{2,1,0:T(8,128)S(1)} %copy-done.1, f32[896,128]{1,0:T(8,128)S(1)} %get-tuple-element.187, f32[16,896]{1,0:T(8,128)S(1)} %fusion.47, bf16[16,128,128]{2,1,0:T(8,128)(2,1)S(1)} %get-tuple-element.185), kind=kOutput, calls=%fused_computation.2.clone.1 | convolution fusion | flops 482607104 | bytes 23060480 | tf_op jit(solution)/shard_map/while/body/eval_jaxpr/svi,sij->svj/dot_general | solution.py:47
  242.8 13.3 %all-gather.3 = f32[64,350]{1,0:T(8,128)S(1)} all-gather(f32[16,350]{1,0:T(8,128)S(1)} %fusion.48), channel_id=2, replica_groups=mesh['scen'=8,'veh'=4] {'veh'}, dimensions={0}, use_global_device_ids=true | all-gather | bytes 112000 | tf_op jit(solution)/shard_map/while/body/eval_jaxpr/all_gather | solution.py:50
  262.8 5.9 %multiply_subtract_fusion.2 = f32[16,896,128]{2,1,0:T(8,128)} fusion(f32[16,896,128]{2,1,0:T(8,128)S(1)} %copy.53, f32[16,896,128]{2,1,0:T(8,128)S(1)} %copy-done.1, f32[896,128]{1,0:T(8,128)S(1)} %get-tuple-element.187, f32[16,896]{1,0:T(8,128)S(1)} %fusion.47, bf16[16,128,128]{2,1,0:T(8,128)(2,1)S(1)} %get-tuple-element.185), kind=kOutput, calls=%fused_computation.2.clone.1 | convolution fusion | flops 482607104 | bytes 23060480 | tf_op jit(solution)/shard_map/while/body/eval_jaxpr/svi,sij->svj/dot_general | solution.py:47
  269.6 13.3 %all-gather.3 = f32[64,350]{1,0:T(8,128)S(1)} all-gather(f32[16,350]{1,0:T(8,128)S(1)} %fusion.48), channel_id=2, replica_groups=mesh['scen'=8,'veh'=4] {'veh'}, dimensions={0}, use_global_device_ids=true | all-gather | bytes 112000 | tf_op jit(solution)/shard_map/while/body/eval_jaxpr/all_gather | solution.py:50
  289.6 5.9 %multiply_subtract_fusion.2 = f32[16,896,128]{2,1,0:T(8,128)} fusion(f32[16,896,128]{2,1,0:T(8,128)S(1)} %copy.53, f32[16,896,128]{2,1,0:T(8,128)S(1)} %copy-done.1, f32[896,128]{1,0:T(8,128)S(1)} %get-tuple-element.187, f32[16,896]{1,0:T(8,128)S(1)} %fusion.47, bf16[16,128,128]{2,1,0:T(8,128)(2,1)S(1)} %get-tuple-element.185), kind=kOutput, calls=%fused_computation.2.clone.1 | convolution fusion | flops 482607104 | bytes 23060480 | tf_op jit(solution)/shard_map/while/body/eval_jaxpr/svi,sij->svj/dot_general | solution.py:47
  296.4 13.2 %all-gather.3 = f32[64,350]{1,0:T(8,128)S(1)} all-gather(f32[16,350]{1,0:T(8,128)S(1)} %fusion.48), channel_id=2, replica_groups=mesh['scen'=8,'veh'=4] {'veh'}, dimensions={0}, use_global_device_ids=true | all-gather | bytes 112000 | tf_op jit(solution)/shard_map/while/body/eval_jaxpr/all_gather | solution.py:50
  316.2 5.9 %multiply_subtract_fusion.2 = f32[16,896,128]{2,1,0:T(8,128)} fusion(f32[16,896,128]{2,1,0:T(8,128)S(1)} %copy.53, f32[16,896,128]{2,1,0:T(8,128)S(1)} %copy-done.1, f32[896,128]{1,0:T(8,128)S(1)} %get-tuple-element.187, f32[16,896]{1,0:T(8,128)S(1)} %fusion.47, bf16[16,128,128]{2,1,0:T(8,128)(2,1)S(1)} %get-tuple-element.185), kind=kOutput, calls=%fused_computation.2.clone.1 | convolution fusion | flops 482607104 | bytes 23060480 | tf_op jit(solution)/shard_map/while/body/eval_jaxpr/svi,sij->svj/dot_general | solution.py:47
  323.1 13.4 %all-gather.3 = f32[64,350]{1,0:T(8,128)S(1)} all-gather(f32[16,350]{1,0:T(8,128)S(1)} %fusion.48), channel_id=2, replica_groups=mesh['scen'=8,'veh'=4] {'veh'}, dimensions={0}, use_global_device_ids=true | all-gather | bytes 112000 | tf_op jit(solution)/shard_map/while/body/eval_jaxpr/all_gather | solution.py:50
  343.1 5.9 %multiply_subtract_fusion.2 = f32[16,896,128]{2,1,0:T(8,128)} fusion(f32[16,896,128]{2,1,0:T(8,128)S(1)} %copy.53, f32[16,896,128]{2,1,0:T(8,128)S(1)} %copy-done.1, f32[896,128]{1,0:T(8,128)S(1)} %get-tuple-element.187, f32[16,896]{1,0:T(8,128)S(1)} %fusion.47, bf16[16,128,128]{2,1,0:T(8,128)(2,1)S(1)} %get-tuple-element.185), kind=kOutput, calls=%fused_computation.2.clone.1 | convolution fusion | flops 482607104 | bytes 23060480 | tf_op jit(solution)/shard_map/while/body/eval_jaxpr/svi,sij->svj/dot_general | solution.py:47
  349.9 13.3 %all-gather.3 = f32[64,350]{1,0:T(8,128)S(1)} all-gather(f32[16,350]{1,0:T(8,128)S(1)} %fusion.48), channel_id=2, replica_groups=mesh['scen'=8,'veh'=4] {'veh'}, dimensions={0}, use_global_device_ids=true | all-gather | bytes 112000 | tf_op jit(solution)/shard_map/while/body/eval_jaxpr/all_gather | solution.py:50
  363.4 14.0 %fusion.14 = f32[8,896,128]{2,0,1:T(8,128)} fusion(f32[16,896,128]{2,1,0:T(8,128)} %get-tuple-element.48, f32[16]{0:T(128)S(1)} %dynamic-slice_convert_fusion.1, s32[16]{0:T(128)S(1)} %dynamic-slice_bitcast_fusion), kind=kOutput, calls=%fused_computation.18 | convolution fusion | flops 176161024 | bytes 11010176 | tf_op jit(solution)/shard_map/sb,svi->bvi/dot_general | solution.py:69
  377.4 5.6 %convert_element_type.49 = bf16[16,896,128]{2,1,0:T(8,128)(2,1)} convert(f32[16,896,128]{2,1,0:T(8,128)} %get-tuple-element.48) | non-fusion elementwise | flops 1835008 | bytes 11010048 | tf_op jit(solution)/shard_map/convert_element_type | solution.py:80
  384.4 69.0 %all-reduce.2.cloned.1.call-done = f32[8,896,128]{2,0,1:T(8,128)} async-done(((f32[8,896,128]{2,0,1:T(8,128)}), f32[8,896,128]{2,0,1:T(8,128)}) %all-reduce.2.cloned.1.call-update) | async-done | bytes 3670032 | tf_op jit(solution)/shard_map/psum | solution.py:70
  456.5 17.2 %multiply_reduce_fusion.1 = (f32[16]{0:T(128)S(1)}, bf16[16,896,128]{2,0,1:T(8,128)(2,1)S(1)}) fusion(bf16[16,896,128]{2,1,0:T(8,128)(2,1)S(1)} %copy-done.3, f32[8,896,128]{2,0,1:T(8,128)S(1)} %broadcast_divide_fusion, s32[16]{0:T(128)S(1)} %dynamic-slice_bitcast_fusion, f32[16,896,128]{2,1,0:T(8,128)} %get-tuple-element.48), kind=kOutput, calls=%fused_computation.17 | convolution fusion | flops 187170928 | bytes 18350208 | tf_op jit(solution)/shard_map/sb,bvi->svi/dot_general | solution.py:73
  477.2 39.5 %psum.15 = f32[]{:T(128)} all-reduce(f32[]{:T(128)} %multiply_reduce_fusion.2), channel_id=1, replica_groups=mesh['scen'=8,'veh'=4] {'scen','veh'}, use_global_device_ids=true, to_apply=%region_8.0 | all-reduce | flops 1 | bytes 8 | tf_op jit(solution)/shard_map/psum | solution.py:77
  (134 shorter events, 106.1 us)
Async XLA Ops:
  7.2 1.5 copy-start
  7.2 446.2 %all-reduce.2.cloned.1.call-start = ((), (), s32[]{:S(2)}) async-start(), calls=%async_computation | async-start | bytes 7340032 | tf_op jit(solution)/shard_map/psum | solution.py:70
  31.3 5.2 copy-start.5
  36.5 3.8 copy-start.9
  36.5 3.8 copy-start.4
  36.5 3.9 copy-start.7
  36.5 3.9 copy-start.8
  36.5 3.9 copy-start.11
  40.4 322.9 %copy-start.10 = (s32[128]{0:T(128)S(1)}, s32[128]{0:T(128)}, u32[]{:S(2)}) copy-start(s32[128]{0:T(128)} %param.23) | copy-start | bytes 1540
  43.5 3.5 copy-start.1
  72.0 3.5 copy-start.1
  98.9 3.5 copy-start.1
  125.6 3.5 copy-start.1
  152.3 3.5 copy-start.1
  179.1 3.5 copy-start.1
  205.8 3.5 copy-start.1
  232.5 3.5 copy-start.1
  259.3 3.5 copy-start.1
  286.1 3.5 copy-start.1
  312.8 3.5 copy-start.1
  339.6 3.5 copy-start.1
  363.3 14.1 %copy-start.6 = (f32[16,350]{1,0:T(8,128)}, f32[16,350]{1,0:T(8,128)S(1)}, u32[]{:S(2)}) copy-start(f32[16,350]{1,0:T(8,128)S(1)} %get-tuple-element.93) | copy-start | bytes 67204
  377.3 6.9 %copy-start.12 = (s32[128,1]{0,1:T(1,128)S(1)}, s32[128,1]{0,1:T(1,128)}, u32[]{:S(2)}) copy-start(s32[128,1]{0,1:T(1,128)} %param.22) | copy-start | bytes 1540
  453.4 3.1 copy-start.3
  456.5 17.2 %copy-start.2 = (f32[8,896,128]{2,0,1:T(8,128)}, f32[8,896,128]{2,0,1:T(8,128)S(1)}, u32[]{:S(2)}) copy-start(f32[8,896,128]{2,0,1:T(8,128)S(1)} %broadcast_divide_fusion) | copy-start | bytes 11010052
Sparse Core Ops, SparseCore 0:
  377.5 75.8 all-reduce.1
